TPU v7x, 256 devices: a whole 4x4x8 slice. The times are simulated.
256 devices in a mesh: req: 8 (over z), row: 8 (over x, core), col: 4 (over y).
Axes of the slice: x: 4, y: 4, z: 8, core: 2. Of those that a mesh axis runs over, the one named last changes fastest.
Arguments:
- hidden: bfloat16 [4096, 2048], P('req'), as said below
- attention_gain: float32 [2048], replicated, may hold values from 0.5 to 2
- query_weight: bfloat16 [2048, 2048], P('row', 'col'), may hold values from -0.125 to 0.125
- key_value_weight: bfloat16 [2048, 4, 128], P('row', 'col'), may hold values from -0.125 to 0.125
- output_weight: bfloat16 [2048, 2048], P('col', 'row'), may hold values from -0.75 to 0.75
- final_gain: float32 [2048], replicated, may hold values from 0.5 to 2
- head_weight: bfloat16 [2048, 32064], P(None, ('row', 'col')), as said below
- key_value_cache: bfloat16 [64, 2048, 4, 128], P(('req', 'row'), None, 'col'), as said below
- parents: int32 [64, 64], P('req'), may hold values from 0 to 62, as said below
- counts: int32 [64], P('req'), may hold values from 32 to 64, as said below
- lengths: int32 [64], P('req'), may hold values from 1 to 32768
- tokens: int32 [64, 64], P('req'), may hold values from 0 to 32063
- accepted_path: int32 [64, 8], P('req'), may hold values from 0 to 28, as said below
- accept_count: int32 [64], P('req'), may hold values from 1 to 8
Outputs:
- node_logprob: float32 [64, 64], P('req')
- next_logprob: float32 [64, 32064], P('req', ('row', 'col'))
- accepted_cache: bfloat16 [64, 8, 4, 128], P(('req', 'row'), None, 'col')
Inputs may be any that keep to these rules, and one draw needn't show every extreme that they name: `hidden`: real values. `head_weight`: real values. `key_value_cache`: real values; slots that the lengths leave empty hold values that must not be used. `parents`: for node i >= 1 the parent is below i and at least i - 4; the entry of node 0 is 0. Nodes 0 to counts[b] - 1 of request b are live, and every ancestor of a live node is live. accepted_path[b, 0] = 0, each entry below accept_count[b] is a live child of the one before, and the entries from accept_count[b] on are 0.
All inputs are finite; a program needn't handle non-finite values.
Results may differ from a plain program's by a relative error of at most 0.0093.
Values may be sent and summed in bfloat16 or wider, within the bound.
A program may use at most 64 MiB of HBM per device.

v0:
```python
import math
import jax
import jax.numpy as jnp
from jax import lax
from jax.sharding import PartitionSpec as P

D = 2048
NODES = 64
epsilon = 1e-05


def combined_all(value, axis, combine):
    everything = jax.tree.map(lambda part: lax.all_gather(part, axis), value)
    initial = jax.tree.map(lambda part: part[0], everything)

    def turn(k, so_far):
        return combine(so_far, jax.tree.map(lambda part: part[k], everything))

    return lax.fori_loop(1, lax.axis_size(axis), turn, initial)


def ancestry(parents):
    node_count = parents.shape[1]
    node_ids = jnp.arange(node_count, dtype=jnp.int32)
    linked = (parents[:, :, None] == node_ids[None, None, :]) & (node_ids[None, :, None] > 0)
    reached = jnp.eye(node_count, dtype=jnp.float32)[None] + linked.astype(jnp.float32)
    for sweep in range(node_count.bit_length()):
        reached = jnp.minimum(
            jnp.einsum("bij,bjk->bik", reached, reached, precision=lax.Precision.HIGHEST), 1.0
        )
    return (reached, jnp.sum(reached, axis=2) - 1.0)


def rotate(values, positions):
    half_size = values.shape[-1] // 2
    frequency = 10000.0 ** (-jnp.arange(half_size, dtype=jnp.float32) / half_size)
    angles = positions[..., None, None] * frequency
    cosine = jnp.cos(angles)
    sine_part = jnp.sin(angles)
    front_half = values[..., :half_size]
    back_half = values[..., half_size:]
    return jnp.concatenate(
        [front_half * cosine - back_half * sine_part, back_half * cosine + front_half * sine_part],
        axis=-1,
    )


def attend(queries, new_keys, new_values, cache_rows, reached, depths, length):
    node_count, head_count, head_size = queries.shape
    group_count = new_keys.shape[1]
    window_size = cache_rows.shape[0]
    grouped = queries.reshape(node_count, group_count, head_count // group_count, head_size)
    all_keys = jnp.concatenate([cache_rows[:, :, :head_size], new_keys], axis=0)
    all_values = jnp.concatenate([cache_rows[:, :, head_size:], new_values], axis=0)
    scores = jnp.einsum("ngqd,kgd->gqnk", grouped, all_keys, preferred_element_type=jnp.float32) * (
        1.0 / math.sqrt(head_size)
    )
    slot_ids = jnp.arange(window_size, dtype=jnp.float32)
    cache_open = (slot_ids[None, :] > depths[:, None]) & (
        slot_ids[None, :] >= (window_size - length).astype(jnp.float32)
    )
    allowed = jnp.concatenate([cache_open, reached > 0.5], axis=1)
    scores = jnp.where(allowed[None, None], scores, -jnp.inf)
    row_max = jnp.max(scores, axis=3, keepdims=True)
    weights = jnp.exp(scores - row_max)
    weights_bf = (weights / jnp.sum(weights, axis=3, keepdims=True)).astype(jnp.bfloat16)
    attended = jnp.einsum(
        "gqnk,kgd->ngqd", weights_bf, all_values, preferred_element_type=jnp.float32
    )
    return attended.reshape(node_count, head_count * head_size).astype(jnp.bfloat16)


def attend_packed(packed):
    return attend(*packed)


def combine_parts(first_part, second_part):
    larger = jnp.maximum(first_part[0], second_part[0])
    summed = first_part[1] * jnp.exp(first_part[0] - larger) + second_part[1] * jnp.exp(
        second_part[0] - larger
    )
    return (larger, summed, first_part[2] + second_part[2])


def shards(
    hidden,
    attention_gain,
    query_weight,
    key_value_weight,
    output_weight,
    final_gain,
    head_weight,
    key_value_cache,
    parents,
    counts,
    lengths,
    tokens,
    accepted_path,
    accept_count,
):
    group_requests = parents.shape[0]
    local_requests = key_value_cache.shape[0]
    row_slot = lax.axis_index("row")
    row_width = query_weight.shape[0]
    query_width = query_weight.shape[1]
    group_count = key_value_weight.shape[1]
    head_size = key_value_weight.shape[2] // 2
    widened = hidden.astype(jnp.float32)
    inverse_norm = lax.rsqrt(jnp.mean(widened * widened, axis=1, keepdims=True) + epsilon)
    wide_part = lax.dynamic_slice_in_dim(widened, row_slot * row_width, row_width, 1)
    pair_weight = key_value_weight.reshape(row_width, group_count * 2 * head_size)
    gain_part = lax.dynamic_slice_in_dim(attention_gain, row_slot * row_width, row_width, 0)
    normed = (wide_part * inverse_norm * gain_part).astype(jnp.bfloat16)
    joint_weight = jnp.concatenate([query_weight, pair_weight], axis=1)
    own_terms = lax.psum_scatter(
        jnp.dot(normed, joint_weight, preferred_element_type=jnp.float32),
        "row",
        scatter_dimension=0,
        tiled=True,
    )
    own_parents = lax.dynamic_slice_in_dim(parents, row_slot * local_requests, local_requests, 0)
    own_lengths = lax.dynamic_slice_in_dim(lengths, row_slot * local_requests, local_requests, 0)
    reached, depths = ancestry(own_parents)
    positions = own_lengths[:, None].astype(jnp.float32) + depths
    raw_queries = own_terms[:, :query_width].reshape(
        local_requests, NODES, query_width // head_size, head_size
    )
    queries = rotate(raw_queries, positions).astype(jnp.bfloat16)
    raw_pairs = own_terms[:, query_width:].reshape(
        local_requests, NODES, group_count, 2 * head_size
    )
    new_keys = rotate(raw_pairs[..., :head_size], positions).astype(jnp.bfloat16)
    new_values = raw_pairs[..., head_size:].astype(jnp.bfloat16)
    attended = lax.map(
        attend_packed,
        (queries, new_keys, new_values, key_value_cache, reached, depths, own_lengths),
    )
    attended = attended.reshape(local_requests * NODES, query_width)
    head_terms = jnp.dot(
        lax.all_gather(attended, "row", axis=0, tiled=True),
        output_weight,
        preferred_element_type=jnp.float32,
    )
    vocab_width = head_weight.shape[1]
    col_share = lax.psum_scatter(head_terms, "col", scatter_dimension=1, tiled=True)
    share_width = col_share.shape[1]
    share_start = row_slot * row_width + lax.axis_index("col") * share_width
    residual = lax.dynamic_slice_in_dim(widened, share_start, share_width, 1) + col_share
    squares = lax.psum(jnp.sum(residual * residual, axis=1), ("row", "col"))
    final_part = lax.dynamic_slice_in_dim(final_gain, share_start, share_width, 0)
    normed_out = (residual * lax.rsqrt(squares / D + epsilon)[:, None] * final_part).astype(
        jnp.bfloat16
    )
    logits = jnp.dot(
        lax.all_gather(normed_out, ("row", "col"), axis=1, tiled=True),
        head_weight,
        preferred_element_type=jnp.float32,
    )
    vocab_start = lax.axis_index(("row", "col")) * vocab_width
    request_base = jnp.arange(group_requests, dtype=jnp.int32)[:, None] * NODES
    parent_rows = (request_base + parents).reshape(-1)
    token_cols = tokens.reshape(-1) - vocab_start
    inside = (token_cols >= 0) & (token_cols < vocab_width)
    picked = jnp.where(inside, logits[parent_rows, jnp.clip(token_cols, 0, vocab_width - 1)], 0.0)
    local_max = jnp.max(logits, axis=1)
    local_total = jnp.sum(jnp.exp(logits - local_max[:, None]), axis=1)
    whole_max, whole_total, whole_pick = combined_all(
        (local_max, local_total, picked), ("row", "col"), combine_parts
    )
    log_total = whole_max + jnp.log(whole_total)
    node_ids = jnp.arange(NODES, dtype=jnp.int32)[None, :]
    live_nodes = (node_ids > 0) & (node_ids < counts[:, None])
    node_scores = (whole_pick - log_total[parent_rows]).reshape(group_requests, NODES)
    node_logprob = jnp.where(live_nodes, node_scores, jnp.zeros_like(node_scores))
    last_nodes = jnp.take_along_axis(accepted_path, (accept_count - 1)[:, None], axis=1)[:, 0]
    last_rows = request_base[:, 0] + last_nodes
    next_logprob = logits[last_rows] - log_total[last_rows][:, None]
    own_path = lax.dynamic_slice_in_dim(accepted_path, row_slot * local_requests, local_requests, 0)
    own_accept = lax.dynamic_slice_in_dim(
        accept_count, row_slot * local_requests, local_requests, 0
    )
    fresh_rows = jnp.concatenate([new_keys, new_values], axis=3)
    chosen_rows = jnp.take_along_axis(fresh_rows, own_path[:, :, None, None], axis=1)
    step_ids = jnp.arange(own_path.shape[1], dtype=jnp.int32)
    kept_rows = (step_ids[None, :] < own_accept[:, None])[:, :, None, None]
    accepted_cache = jnp.where(kept_rows, chosen_rows, jnp.zeros_like(chosen_rows))
    return (node_logprob, next_logprob, accepted_cache)


def solution(mesh):
    in_specs = (
        P("req", None),
        P(),
        P("row", "col"),
        P("row", "col", None),
        P("col", "row"),
        P(),
        P(None, ("row", "col")),
        P(("req", "row"), None, "col", None),
        P("req", None),
        P("req"),
        P("req"),
        P("req", None),
        P("req", None),
        P("req"),
    )
    out_specs = (P("req", None), P("req", ("row", "col")), P(("req", "row"), None, "col", None))
    return jax.shard_map(shards, mesh=mesh, in_specs=in_specs, out_specs=out_specs, check_vma=False)
```

profile of v0, /device:TPU:32, one launch (start us, length us, event | category | flops | bytes accessed | tf_op | source)
XLA Modules:
  0.0 367.7 jit_solution(17106997792936549415)
XLA Ops:
  7.2 2.9 copy.31
  10.2 0.5 multiply_reduce_fusion
  10.7 2.5 convert_element_type.107
  13.2 0.8 dynamic_slice.78
  14.0 2.6 fusion.9
  16.7 0.2 fusion.28
  16.9 0.2 convolution_minimum_fusion.6
  17.1 0.2 convolution_minimum_fusion.5
  17.3 0.2 convolution_minimum_fusion.4
  17.4 0.2 convolution_minimum_fusion.3
  17.6 0.6 dynamic_slice.81
  19.5 0.2 copy.32
  19.7 0.2 convolution_minimum_fusion.2
  19.9 0.2 convolution_minimum_fusion.1
  20.1 0.2 broadcast_compare_fusion
  20.2 0.1 reduce_sum.47
  20.4 0.2 multiply_cosine_fusion
  20.6 0.2 fusion.8
  20.8 33.7 %reduce-scatter.3.cloned.1.call-done = f32[64,640]{1,0:T(8,128)} async-done(((f32[512,640]{1,0:T(8,128)}), f32[64,640]{1,0:T(8,128)}) %reduce-scatter.3.cloned.1.call-update) | async-done | bytes 163856 | tf_op jit(solution)/shard_map/reduce_scatter | solution.py:115
  54.5 0.8 slice_bitcast_fusion
  55.2 0.1 slice_bitcast_fusion.1
  55.3 0.2 fusion.30
  55.5 0.1 copy.33
  55.6 0.1 pad_maximum_fusion
  55.7 0.1 copy.34
  55.8 0.9 slice.77
  56.7 0.1 reshape.755
  56.8 0.1 fusion.48
  57.0 0.1 fusion.19
  57.1 1.0 fusion.49
  58.1 0.7 fusion.2
  58.9 1.4 fusion.5
  60.2 0.1 copy.37
  60.3 13.1 %all_gather.22 = bf16[512,512]{1,0:T(8,128)(2,1)S(1)} all-gather(bf16[64,512]{1,0:T(8,128)(2,1)S(1)} %copy.37), channel_id=1, replica_groups=mesh['req'=8,'row'=8,'col'=4] {'row'}, dimensions={0}, use_global_device_ids=true | all-gather | bytes 589824 | tf_op jit(solution)/shard_map/all_gather | solution.py:140
  73.5 1.1 fusion.51
  74.7 0.8 dynamic_slice.82
  75.4 23.3 %reduce-scatter.5.cloned.1.call-done = f32[512,64]{0,1:T(8,128)} async-done(((f32[512,256]{0,1:T(8,128)}), f32[512,64]{0,1:T(8,128)}) %reduce-scatter.5.cloned.1.call-update) | async-done | bytes 131088 | tf_op jit(solution)/shard_map/reduce_scatter | solution.py:145
  98.8 1.0 multiply_reduce_fusion.1
  99.8 63.2 %psum.7 = f32[512]{0:T(512)S(1)} all-reduce(f32[512]{0:T(512)S(1)} %multiply_reduce_fusion.1), channel_id=1, replica_groups=mesh['req'=8,'row'=8,'col'=4] {'row','col'}, use_global_device_ids=true, to_apply=%region_7.8 | all-reduce | flops 512 | bytes 4096 | tf_op jit(solution)/shard_map/psum | solution.py:149
  163.0 1.7 multiply_convert_fusion.2
  164.7 0.6 dynamic_slice.83
  165.3 0.1 and.87
  165.4 0.1 min.47
  165.5 0.1 reshape.757
  165.7 0.6 gather_fusion.5
  166.3 0.7 iota_compare_fusion.3
  167.1 0.1 slice.91
  167.1 0.1 maximum_bitcast_fusion.4
  167.2 0.6 gather_fusion.4
  167.8 0.7 fusion.38
  168.4 42.6 %all-gather.7.cloned.1.call-done = bf16[512,2048]{0,1:T(8,128)(2,1)} async-done(((bf16[512,64]{0,1:T(8,128)(2,1)}), bf16[512,2048]{0,1:T(8,128)(2,1)}) %all-gather.7.cloned.1.call-update) | async-done | bytes 2097168 | tf_op jit(solution)/shard_map/all_gather | solution.py:155
  211.0 5.1 %fusion.50 = (f32[512]{0:T(512)S(1)}, f32[512,1002]{0,1:T(8,128)S(1)}) fusion(bf16[512,2048]{0,1:T(8,128)(2,1)} %all-gather.7.cloned.1.call-done, bf16[2048,1002]{0,1:T(8,128)(2,1)} %param.22), kind=kOutput, calls=%fused_computation.126 | convolution fusion | flops 2101858816 | bytes 8255488 | tf_op jit(solution)/shard_map/dot_general | solution.py:154
  216.2 1.9 copy.38
  218.0 0.4 exponential_reduce_fusion
  218.4 42.8 %all-gather.3 = f32[32,1,512]{2,1,0:T(1,128)S(1)} all-gather(f32[1,1,512]{2,1,0:T(1,128)S(1)} %bitcast.127), channel_id=3, replica_groups=mesh['req'=8,'row'=8,'col'=4] {'row','col'}, dimensions={0}, use_global_device_ids=true | all-gather | bytes 67584 | tf_op jit(solution)/shard_map/all_gather | solution.py:13
  261.2 4.5 %gather_fusion = f32[512]{0:T(512)S(1)} fusion(f32[512,1002]{0,1:T(8,128)S(1)} %get-tuple-element.248, s32[512]{0:T(512)S(1)} %bitcast.108), kind=kCustom, calls=%fused_computation | custom fusion | bytes 8192 | tf_op jit(solution)/shard_map/gather | solution.py:164
  265.7 41.7 %all-gather.4 = f32[32,1,512]{2,1,0:T(1,128)S(1)} all-gather(f32[1,1,512]{2,1,0:T(1,128)S(1)} %select_bitcast_fusion), channel_id=1, replica_groups=mesh['req'=8,'row'=8,'col'=4] {'row','col'}, dimensions={0}, use_global_device_ids=true | all-gather | bytes 67584 | tf_op jit(solution)/shard_map/all_gather | solution.py:13
  307.4 43.1 %all-gather.2 = f32[32,1,512]{2,1,0:T(1,128)S(1)} all-gather(f32[1,1,512]{2,1,0:T(1,128)S(1)} %bitcast.125), channel_id=2, replica_groups=mesh['req'=8,'row'=8,'col'=4] {'row','col'}, dimensions={0}, use_global_device_ids=true | all-gather | bytes 67584 | tf_op jit(solution)/shard_map/all_gather | solution.py:13
  350.5 2.9 while.23
  353.4 2.2 gather_fusion.2
  355.6 0.6 gather_fusion.3
  356.2 3.5 gather_fusion.1
  359.8 0.7 broadcast_subtract_fusion
  360.5 0.7 fusion.34
  (184 shorter events, 2.4 us)
Async XLA Ops:
  7.2 66.3 %copy-start = (bf16[512,256]{1,0:T(8,128)(2,1)S(1)}, bf16[512,256]{1,0:T(8,128)(2,1)}, u32[]{:S(2)}) copy-start(bf16[512,256]{1,0:T(8,128)(2,1)} %param.20) | copy-start | bytes 786436
  7.2 47.3 %reduce-scatter.3.cloned.1.call-start = ((), (), s32[]{:S(2)}) async-start(), calls=%async_computation.2 | async-start | bytes 1474560 | tf_op jit(solution)/shard_map/reduce_scatter | solution.py:115
  10.1 3.9 %copy-start.3 = (bf16[256,512]{1,0:T(8,128)(2,1)S(1)}, bf16[256,512]{1,0:T(8,128)(2,1)}, u32[]{:S(2)}) copy-start(bf16[256,512]{1,0:T(8,128)(2,1)} %param.18) | copy-start | bytes 786436
  10.1 3.9 %copy-start.4 = (bf16[256,1,128]{2,0,1:T(8,128)(2,1)S(1)}, bf16[256,1,128]{2,0,1:T(8,128)(2,1)}, u32[]{:S(2)}) copy-start(bf16[256,1,128]{2,0,1:T(8,128)(2,1)} %param.19) | copy-start | bytes 196612
  10.7 6.0 %copy-start.6 = (s32[8,64]{1,0:T(8,128)S(1)}, s32[8,64]{1,0:T(8,128)}, u32[]{:S(2)}) copy-start(s32[8,64]{1,0:T(8,128)} %param.24) | copy-start | bytes 6148
  10.7 6.9 %copy-start.8 = (s32[8]{0:T(128)S(1)}, s32[8]{0:T(128)}, u32[]{:S(2)}) copy-start(s32[8]{0:T(128)} %param.26) | copy-start | bytes 100
  10.7 8.8 %copy-start.2 = (bf16[1,2048,1,128]{3,1,2,0:T(8,128)(2,1)S(1)}, bf16[1,2048,1,128]{3,1,2,0:T(8,128)(2,1)}, u32[]{:S(2)}) copy-start(bf16[1,2048,1,128]{3,1,2,0:T(8,128)(2,1)} %param.23) | copy-start | bytes 1572868
  16.6 82.1 %reduce-scatter.5.cloned.1.call-start = ((), (), s32[]{:S(2)}) async-start(), calls=%async_computation.3 | async-start | bytes 655360 | tf_op jit(solution)/shard_map/reduce_scatter | solution.py:145
  58.8 105.9 %copy-start.9 = (s32[8]{0:T(128)S(1)}, s32[8]{0:T(128)}, u32[]{:S(2)}) copy-start(s32[8]{0:T(128)} %param.29) | copy-start | bytes 100
  58.8 106.4 %copy-start.5 = (s32[8,64]{1,0:T(8,128)S(1)}, s32[8,64]{1,0:T(8,128)}, u32[]{:S(2)}) copy-start(s32[8,64]{1,0:T(8,128)} %param.27) | copy-start | bytes 6148
  58.8 106.8 %copy-start.1 = (s32[8,8]{1,0:T(8,128)S(1)}, s32[8,8]{1,0:T(8,128)}, u32[]{:S(2)}) copy-start(s32[8,8]{1,0:T(8,128)} %param.28) | copy-start | bytes 772
  74.6 136.4 %all-gather.7.cloned.1.call-start = ((), (), s32[]{:S(2)}) async-start(), calls=%async_computation.4 | async-start | bytes 2162688 | tf_op jit(solution)/shard_map/all_gather | solution.py:155
  218.0 142.5 %copy-start.7 = (s32[8]{0:T(128)S(1)}, s32[8]{0:T(128)}, u32[]{:S(2)}) copy-start(s32[8]{0:T(128)} %param.25) | copy-start | bytes 100
Sparse Core Ops, SparseCore 0:
  16.7 37.6 reduce-scatter.2
  74.7 23.9 reduce-scatter.4
  164.8 46.2 all-gather.6
where the time goes:
time: 368 us
  blocking collectives  204 us (55%)
  waiting for transfers between devices  99.6 us (27%)
  local copies, waits for them, and re-layouts  23.3 us (6%)
  between operations  15.5 us (4%)
  matrix products  12.4 us (3%)
  other arithmetic  11.8 us (3%)
    all_gather x3, blocking collectives, combined_all(): everything = jax.tree.map(lambda part: lax.all_gather(part, axis), value)  128 us
    psum x1, blocking collectives, shards(): squares = lax.psum(jnp.sum(residual * residual, axis=1), ('row', 'col'))  63.2 us
    all_gather x1, waiting for transfers between devices, shards(): lax.all_gather(normed_out, ('row', 'col'), axis=1, tiled=True)  42.6 us
    reduce_scatter x1, waiting for transfers between devices, shards(): lax.psum_scatter(jnp.dot(normed, joint_weight, preferred_element_type=jnp...  33.7 us
    reduce_scatter x1, waiting for transfers between devices, shards(): lax.psum_scatter(head_terms, 'col', scatter_dimension=1, tiled=True)  23.3 us
    all_gather x1, blocking collectives, shards(): lax.all_gather(attended, 'row', axis=0, tiled=True)  13.1 us
  transfers between devices with their start and end apart: 3, of which 3 were waited for; matrix products, arithmetic and copies ran while one was open for 2% of the time, Pallas kernels for 0%

commit v1 on v0

--- a/solution.py
+++ b/solution.py
@@ -146,7 +146,7 @@
     share_width = col_share.shape[1]
     share_start = row_slot * row_width + lax.axis_index("col") * share_width
     residual = lax.dynamic_slice_in_dim(widened, share_start, share_width, 1) + col_share
-    squares = lax.psum(jnp.sum(residual * residual, axis=1), ("row", "col"))
+    squares = jnp.sum(lax.all_gather(jnp.sum(residual * residual, axis=1), ("row", "col")), axis=0)
     final_part = lax.dynamic_slice_in_dim(final_gain, share_start, share_width, 0)
     normed_out = (residual * lax.rsqrt(squares / D + epsilon)[:, None] * final_part).astype(
         jnp.bfloat16

time: 368 us -> 348 us (0.946)
  blocking collectives: 204 us -> 182 us
    psum x1 -> x0, blocking collectives: 63.2 us -> none  [shards(): squares = lax.psum(jnp.sum(residual * residual, axis=1), ('row', 'col'))]
    all_gather x0 -> x1, blocking collectives: none -> 41.1 us  [shards(): lax.all_gather(jnp.sum(residual * residual, axis=1), ('row', 'col'))]
where the time goes in v1:
time: 348 us
  blocking collectives  182 us (52%)
  waiting for transfers between devices  102 us (29%)
  local copies, waits for them, and re-layouts  23.3 us (7%)
  between operations  15.5 us (4%)
  matrix products  12.4 us (4%)
  other arithmetic  11.9 us (3%)
    all_gather x3, blocking collectives, combined_all(): everything = jax.tree.map(lambda part: lax.all_gather(part, axis), value)  128 us
    all_gather x1, waiting for transfers between devices, shards(): lax.all_gather(normed_out, ('row', 'col'), axis=1, tiled=True)  44.7 us
    all_gather x1, blocking collectives, shards(): lax.all_gather(jnp.sum(residual * residual, axis=1), ('row', 'col'))  41.1 us
    reduce_scatter x1, waiting for transfers between devices, shards(): lax.psum_scatter(jnp.dot(normed, joint_weight, preferred_element_type=jnp...  33.7 us
    reduce_scatter x1, waiting for transfers between devices, shards(): lax.psum_scatter(head_terms, 'col', scatter_dimension=1, tiled=True)  23.3 us
    all_gather x1, blocking collectives, shards(): lax.all_gather(attended, 'row', axis=0, tiled=True)  13.1 us
  transfers between devices with their start and end apart: 3, of which 3 were waited for; matrix products, arithmetic and copies ran while one was open for 2% of the time, Pallas kernels for 0%

profile of v1, /device:TPU:32, one launch (start us, length us, event | category | flops | bytes accessed | tf_op | source)
XLA Modules:
  0.0 347.7 jit_solution(2057458996931034561)
XLA Ops:
  7.2 2.9 copy.31
  10.2 0.5 multiply_reduce_fusion
  10.7 2.5 convert_element_type.107
  13.2 0.8 dynamic_slice.78
  14.0 2.6 fusion.9
  16.7 0.2 fusion.28
  16.9 0.2 convolution_minimum_fusion.6
  17.1 0.2 convolution_minimum_fusion.5
  17.3 0.2 convolution_minimum_fusion.4
  17.4 0.2 convolution_minimum_fusion.3
  17.6 0.6 dynamic_slice.81
  19.5 0.2 copy.32
  19.7 0.2 convolution_minimum_fusion.2
  19.9 0.2 convolution_minimum_fusion.1
  20.1 0.2 broadcast_compare_fusion
  20.2 0.1 reduce_sum.56
  20.4 0.2 multiply_cosine_fusion
  20.6 0.2 fusion.8
  20.8 33.7 %reduce-scatter.3.cloned.1.call-done = f32[64,640]{1,0:T(8,128)} async-done(((f32[512,640]{1,0:T(8,128)}), f32[64,640]{1,0:T(8,128)}) %reduce-scatter.3.cloned.1.call-update) | async-done | bytes 163856 | tf_op jit(solution)/shard_map/reduce_scatter | solution.py:115
  54.5 0.8 slice_bitcast_fusion
  55.2 0.1 slice_bitcast_fusion.1
  55.3 0.2 fusion.30
  55.5 0.1 copy.33
  55.6 0.1 pad_maximum_fusion
  55.7 0.1 copy.34
  55.8 0.9 slice.77
  56.7 0.1 reshape.759
  56.8 0.1 fusion.48
  57.0 0.1 fusion.19
  57.1 1.0 fusion.49
  58.1 0.7 fusion.2
  58.9 1.4 fusion.5
  60.2 0.1 copy.37
  60.3 13.1 %all_gather.28 = bf16[512,512]{1,0:T(8,128)(2,1)S(1)} all-gather(bf16[64,512]{1,0:T(8,128)(2,1)S(1)} %copy.37), channel_id=1, replica_groups=mesh['req'=8,'row'=8,'col'=4] {'row'}, dimensions={0}, use_global_device_ids=true | all-gather | bytes 589824 | tf_op jit(solution)/shard_map/all_gather | solution.py:140
  73.5 1.1 fusion.51
  74.7 0.8 dynamic_slice.82
  75.4 23.3 %reduce-scatter.5.cloned.1.call-done = f32[512,64]{0,1:T(8,128)} async-done(((f32[512,256]{0,1:T(8,128)}), f32[512,64]{0,1:T(8,128)}) %reduce-scatter.5.cloned.1.call-update) | async-done | bytes 131088 | tf_op jit(solution)/shard_map/reduce_scatter | solution.py:145
  98.8 1.0 multiply_reduce_fusion.1
  99.8 41.1 %all-gather.3 = f32[32,1,512]{2,1,0:T(1,128)S(1)} all-gather(f32[1,1,512]{2,1,0:T(1,128)S(1)} %bitcast.125), channel_id=2, replica_groups=mesh['req'=8,'row'=8,'col'=4] {'row','col'}, dimensions={0}, use_global_device_ids=true | all-gather | bytes 67584 | tf_op jit(solution)/shard_map/all_gather | solution.py:149
  140.9 1.7 multiply_convert_fusion.2
  142.6 0.6 dynamic_slice.83
  143.2 0.1 and.87
  143.3 0.1 min.47
  143.5 0.1 reshape.761
  143.6 0.6 gather_fusion.5
  144.3 0.7 iota_compare_fusion.3
  145.0 0.1 slice.91
  145.1 0.1 maximum_bitcast_fusion.4
  145.2 0.6 gather_fusion.4
  145.7 0.7 fusion.38
  146.4 44.7 %all-gather.9.cloned.1.call-done = bf16[512,2048]{0,1:T(8,128)(2,1)} async-done(((bf16[512,64]{0,1:T(8,128)(2,1)}), bf16[512,2048]{0,1:T(8,128)(2,1)}) %all-gather.9.cloned.1.call-update) | async-done | bytes 2097168 | tf_op jit(solution)/shard_map/all_gather | solution.py:155
  191.1 5.1 %fusion.50 = (f32[512]{0:T(512)S(1)}, f32[512,1002]{0,1:T(8,128)S(1)}) fusion(bf16[512,2048]{0,1:T(8,128)(2,1)} %all-gather.9.cloned.1.call-done, bf16[2048,1002]{0,1:T(8,128)(2,1)} %param.22), kind=kOutput, calls=%fused_computation.126 | convolution fusion | flops 2101858816 | bytes 8255488 | tf_op jit(solution)/shard_map/dot_general | solution.py:154
  196.2 1.9 copy.38
  198.0 0.4 exponential_reduce_fusion
  198.4 42.8 %all-gather.5 = f32[32,1,512]{2,1,0:T(1,128)S(1)} all-gather(f32[1,1,512]{2,1,0:T(1,128)S(1)} %bitcast.129), channel_id=4, replica_groups=mesh['req'=8,'row'=8,'col'=4] {'row','col'}, dimensions={0}, use_global_device_ids=true | all-gather | bytes 67584 | tf_op jit(solution)/shard_map/all_gather | solution.py:13
  241.2 4.5 %gather_fusion = f32[512]{0:T(512)S(1)} fusion(f32[512,1002]{0,1:T(8,128)S(1)} %get-tuple-element.248, s32[512]{0:T(512)S(1)} %bitcast.109), kind=kCustom, calls=%fused_computation | custom fusion | bytes 8192 | tf_op jit(solution)/shard_map/gather | solution.py:164
  245.8 41.7 %all-gather.6 = f32[32,1,512]{2,1,0:T(1,128)S(1)} all-gather(f32[1,1,512]{2,1,0:T(1,128)S(1)} %select_bitcast_fusion), channel_id=1, replica_groups=mesh['req'=8,'row'=8,'col'=4] {'row','col'}, dimensions={0}, use_global_device_ids=true | all-gather | bytes 67584 | tf_op jit(solution)/shard_map/all_gather | solution.py:13
  287.4 43.1 %all-gather.4 = f32[32,1,512]{2,1,0:T(1,128)S(1)} all-gather(f32[1,1,512]{2,1,0:T(1,128)S(1)} %bitcast.127), channel_id=3, replica_groups=mesh['req'=8,'row'=8,'col'=4] {'row','col'}, dimensions={0}, use_global_device_ids=true | all-gather | bytes 67584 | tf_op jit(solution)/shard_map/all_gather | solution.py:13
  330.5 2.9 while.23
  333.4 2.2 gather_fusion.2
  335.6 0.6 gather_fusion.3
  336.2 3.5 %gather_fusion.1 = f32[512]{0:T(512)S(1)} fusion(f32[512]{0:T(512)S(1)} %log_add_fusion, s32[1024]{0:T(1024)S(1)} %pad_clamp_fusion.2), kind=kCustom, calls=%fused_computation.1 | custom fusion | bytes 6144 | tf_op jit(solution)/shard_map/gather | solution.py:173
  339.8 0.7 broadcast_subtract_fusion
  340.5 0.7 fusion.34
  (185 shorter events, 2.4 us)
Async XLA Ops:
  7.2 66.3 %copy-start = (bf16[512,256]{1,0:T(8,128)(2,1)S(1)}, bf16[512,256]{1,0:T(8,128)(2,1)}, u32[]{:S(2)}) copy-start(bf16[512,256]{1,0:T(8,128)(2,1)} %param.20) | copy-start | bytes 786436
  7.2 47.3 %reduce-scatter.3.cloned.1.call-start = ((), (), s32[]{:S(2)}) async-start(), calls=%async_computation.2 | async-start | bytes 1474560 | tf_op jit(solution)/shard_map/reduce_scatter | solution.py:115
  10.1 3.9 %copy-start.3 = (bf16[256,512]{1,0:T(8,128)(2,1)S(1)}, bf16[256,512]{1,0:T(8,128)(2,1)}, u32[]{:S(2)}) copy-start(bf16[256,512]{1,0:T(8,128)(2,1)} %param.18) | copy-start | bytes 786436
  10.1 3.9 %copy-start.4 = (bf16[256,1,128]{2,0,1:T(8,128)(2,1)S(1)}, bf16[256,1,128]{2,0,1:T(8,128)(2,1)}, u32[]{:S(2)}) copy-start(bf16[256,1,128]{2,0,1:T(8,128)(2,1)} %param.19) | copy-start | bytes 196612
  10.7 6.0 %copy-start.6 = (s32[8,64]{1,0:T(8,128)S(1)}, s32[8,64]{1,0:T(8,128)}, u32[]{:S(2)}) copy-start(s32[8,64]{1,0:T(8,128)} %param.24) | copy-start | bytes 6148
  10.7 6.9 %copy-start.8 = (s32[8]{0:T(128)S(1)}, s32[8]{0:T(128)}, u32[]{:S(2)}) copy-start(s32[8]{0:T(128)} %param.26) | copy-start | bytes 100
  10.7 8.8 %copy-start.2 = (bf16[1,2048,1,128]{3,1,2,0:T(8,128)(2,1)S(1)}, bf16[1,2048,1,128]{3,1,2,0:T(8,128)(2,1)}, u32[]{:S(2)}) copy-start(bf16[1,2048,1,128]{3,1,2,0:T(8,128)(2,1)} %param.23) | copy-start | bytes 1572868
  16.6 82.1 %reduce-scatter.5.cloned.1.call-start = ((), (), s32[]{:S(2)}) async-start(), calls=%async_computation.3 | async-start | bytes 655360 | tf_op jit(solution)/shard_map/reduce_scatter | solution.py:145
  58.8 83.8 %copy-start.9 = (s32[8]{0:T(128)S(1)}, s32[8]{0:T(128)}, u32[]{:S(2)}) copy-start(s32[8]{0:T(128)} %param.29) | copy-start | bytes 100
  58.8 84.4 %copy-start.5 = (s32[8,64]{1,0:T(8,128)S(1)}, s32[8,64]{1,0:T(8,128)}, u32[]{:S(2)}) copy-start(s32[8,64]{1,0:T(8,128)} %param.27) | copy-start | bytes 6148
  58.8 84.7 %copy-start.1 = (s32[8,8]{1,0:T(8,128)S(1)}, s32[8,8]{1,0:T(8,128)}, u32[]{:S(2)}) copy-start(s32[8,8]{1,0:T(8,128)} %param.28) | copy-start | bytes 772
  74.6 116.4 %all-gather.9.cloned.1.call-start = ((), (), s32[]{:S(2)}) async-start(), calls=%async_computation.4 | async-start | bytes 2162688 | tf_op jit(solution)/shard_map/all_gather | solution.py:155
  198.0 142.5 %copy-start.7 = (s32[8]{0:T(128)S(1)}, s32[8]{0:T(128)}, u32[]{:S(2)}) copy-start(s32[8]{0:T(128)} %param.25) | copy-start | bytes 100
Sparse Core Ops, SparseCore 0:
  16.7 37.6 reduce-scatter.2
  74.7 23.9 reduce-scatter.4
  142.7 48.2 all-gather.8
